TPU v7x, 32 devices: a whole 2x2x4 slice. The times are simulated.
32 devices in a mesh: pole: 4 (over z), row: 4 (over y, x), col: 2 (over core).
Axes of the slice: x: 2, y: 2, z: 4, core: 2. Of those that a mesh axis runs over, the one named last changes fastest.
Arguments:
- green_blocks: bfloat16 [16, 2, 192, 1536], P('pole', 'col', None, 'row'), parts along dimension 0, may hold values from -0.15625 to 0.15625
- lower_panel: bfloat16 [1536, 32, 128], P(('row', 'col'), 'pole'), parts along dimension 1, may hold values from -1.5 to 1.5
- pattern: int32 [12, 8], replicated, may hold values 0 or 1
- pivot_inverse: float32 [8, 512, 128], P(('row', 'col'), 'pole'), parts along dimension 1, may hold values from -6 to 6
Outputs:
- green_panel: bfloat16 [6144, 8, 128], P('pole', ('row', 'col')), parts along dimension 0
- green_diag: float32 [8, 512, 128], P(('row', 'col'), 'pole'), parts along dimension 1
There are 4 independent parts, one for each index of `pole`. A program takes and returns all parts, laid end to end along the dimension named above; an argument that names none is the same for every part. Nothing has to cross between parts.
All inputs are finite; a program needn't handle non-finite values.
Results may differ from a plain program's by a relative error of at most 0.01.
Values may be sent and summed in bfloat16 or wider, within the bound.
A program may use at most 128 MiB of HBM per device.

v0:
```python
import functools
import math

import jax
import jax.numpy as jnp
from jax import lax
from jax.experimental import pallas as pl
from jax.experimental.pallas import tpu as pltpu
from jax.sharding import PartitionSpec as P

MESH = pl.DeviceIdType.MESH
PAIR = 2


def exchange(
    rows, cols, pattern_hbm, green_hbm, panel_hbm, pivot_hbm,
    base, last, column, diag_ref, flags,
    pattern_ref, green_ref, panel_ref, wide, pivot_ref, slab, to_far, from_far, to_x, to_y, to_own, from_own, from_x, from_y,
    load, slab_send, slab_recv, column_send, column_recv, far_send, far_recv,
    x_send, x_recv, y_send, y_recv, own_send, own_recv,
):
    r, c = lax.axis_index("row"), lax.axis_index("col")
    me = r * cols + c
    share, supernodes, width = panel_ref.shape
    mid = rows // 2
    half = mid * share
    row_x, row_y, row_far = r + 1 - 2 * (r % 2), (r + 2) % 4, 3 - r

    def remote(src, dst, send, recv, row, col):
        return pltpu.make_async_remote_copy(
            src_ref=src, dst_ref=dst, send_sem=send, recv_sem=recv,
            device_id={"row": row, "col": col}, device_id_type=MESH,
        )

    barrier = pltpu.get_barrier_semaphore()
    for row in (row_x, row_y):
        for k in range(cols):
            pl.semaphore_signal(barrier, 1, device_id={"row": row, "col": k}, device_id_type=MESH)
    for step in range(1, cols):
        pl.semaphore_signal(barrier, 1, device_id={"row": r, "col": (c + step) % cols}, device_id_type=MESH)
    loads = [
        pltpu.make_async_copy(panel_hbm, panel_ref, load.at[0]),
        pltpu.make_async_copy(green_hbm, green_ref, load.at[1]),
        pltpu.make_async_copy(pivot_hbm, pivot_ref, load.at[2]),
        pltpu.make_async_copy(pattern_hbm, pattern_ref, load.at[3]),
    ]
    for copy in loads:
        copy.start()

    loads[0].wait()
    loads[3].wait()
    wide[...] = panel_ref[...].astype(jnp.float32).reshape(share * supernodes, width)
    piece = math.gcd(share, width)
    for k in range(supernodes):
        value = wide[pl.ds(k, share, stride=supernodes), :]
        parts = []
        for q in range(share // piece):
            flag = pattern_ref[k, (me * share + q * piece) // width].astype(jnp.float32)
            parts.append(value[q * piece:(q + 1) * piece] * flag)
        slab[c, k] = jnp.concatenate(parts, axis=0).astype(jnp.bfloat16)
    pl.semaphore_wait(barrier, 3 * cols - 1)

    started = []

    def start(copy):
        copy.start()
        started.append(copy)

    for step in range(1, cols):
        k = (c + step) % cols
        start(remote(slab.at[c], slab.at[c], slab_send.at[k], slab_recv.at[c], r, k))

    def send_column(d, row):
        for k in range(cols):
            start(remote(
                slab.at[c, row * cols + k], column.at[me],
                column_send.at[d, k], column_recv.at[d, c], row, k,
            ))

    send_column(0, row_x)
    send_column(1, row_y)
    loads[1].wait()

    for step in range(1, cols):
        k = (c + step) % cols
        remote(slab.at[k], slab.at[k], slab_send.at[k], slab_recv.at[k], r, k).wait_recv()

    def product(h, row, k):
        rhs = jnp.concatenate(
            [
                jnp.concatenate([slab[s, row * cols + k + p] for s in range(cols)], axis=0)
                for p in range(PAIR)
            ],
            axis=1,
        )
        lhs = green_ref[h * mid:(h + 1) * mid].reshape(half, green_ref.shape[2])
        value = jnp.dot(lhs, rhs, preferred_element_type=jnp.float32).astype(jnp.bfloat16)
        return value.reshape(mid, share, PAIR * width)

    def fill(buffer, h, row, offset):
        def body(k):
            value = product(h, row, k)
            for p in range(PAIR):
                buffer[k + p, offset:offset + mid] = value[:, :, p * width:(p + 1) * width]

        if cols == PAIR:
            body(0)
        else:
            lax.fori_loop(0, cols // PAIR, lambda i, z: (body(i * PAIR), z)[1], 0)

    for h, row in enumerate((row_x, row_y)):
        fill(to_far.at[h], h, row_far, 0)
        start(remote(to_far.at[h], from_far.at[h], far_send.at[h], far_recv.at[h], row, c))

    def send_direct(buffer, target, send, recv, h, row):
        for k in range(cols):
            start(remote(
                buffer.at[k, pl.ds(h * mid, mid)], target.at[c],
                send.at[h, k], recv.at[h, c], row, k,
            ))

    def send_sum(buffer, send, recv, h, row):
        for k in range(cols):
            start(remote(
                buffer.at[k, pl.ds(h * mid, mid)], last.at[pl.ds(h * mid, mid), c],
                send.at[h, k], recv.at[h, c], row, k,
            ))

    fill(to_x, 0, row_x, 0)
    send_direct(to_x, from_x, x_send, x_recv, 0, row_x)
    fill(to_y, 1, row_y, mid)
    send_direct(to_y, from_y, y_send, y_recv, 1, row_y)
    fill(to_y, 0, row_y, 0)
    fill(to_x, 1, row_x, mid)
    for h in range(2):
        fill(to_own, h, r, h * mid)
    for step in range(1, cols):
        k = (c + step) % cols
        start(remote(to_own.at[k], from_own.at[c], own_send.at[k], own_recv.at[c], r, k))
    from_own[c] = to_own[c]

    for h, row, buffer, send, recv, target in (
        (0, row_x, to_y, y_send, y_recv, row_y), (1, row_y, to_x, x_send, x_recv, row_x)
    ):
        remote(to_far.at[h], from_far.at[h], far_send.at[h], far_recv.at[h], row, c).wait_recv()
        if h == 0:
            send_column(2, row_far)
        for k in range(cols):
            span = slice(h * mid, (h + 1) * mid)
            total = buffer[k, span].astype(jnp.float32) + from_far[h, k].astype(jnp.float32)
            buffer[k, span] = total.astype(jnp.bfloat16)
        send_sum(buffer, send, recv, h, target)

    for s in range(cols):
        column[r * cols + s] = slab[s, me]
    for i in range(flags.shape[0]):
        flags[i] = jnp.broadcast_to(pattern_ref[me, i].astype(jnp.float32), flags.shape[1:])
    for d, row in enumerate((row_x, row_y, row_far)):
        for k in range(cols):
            place = column.at[row * cols + k]
            remote(place, place, column_send.at[d, k], column_recv.at[d, k], row, k).wait_recv()
    for step in range(1, cols):
        k = (c + step) % cols
        remote(to_own.at[k], from_own.at[k], own_send.at[k], own_recv.at[k], r, k).wait_recv()
    loads[2].wait()
    grown = pivot_ref[...]
    for h, source, send, recv, row in ((0, from_x, x_send, x_recv, row_x), (1, from_y, y_send, y_recv, row_y)):
        for k in range(cols):
            remote(source.at[k], source.at[k], send.at[h, k], recv.at[h, k], row, k).wait_recv()
        for j in range(mid):
            panel = []
            value = []
            for s in range(cols):
                value.append(
                    from_own[s, h * mid + j].astype(jnp.float32) + source[s, j].astype(jnp.float32)
                )
                panel.append(column[(h * mid + j) * cols + s])
                base[h * mid + j, s] = value[-1]
            value = jnp.concatenate(value, axis=0)
            high = value.astype(jnp.bfloat16)
            low = (value - high.astype(jnp.float32)).astype(jnp.bfloat16)
            both = lax.dot_general(
                jnp.concatenate(panel, axis=0), jnp.concatenate([high, low], axis=1),
                (((0,), (0,)), ((), ())), preferred_element_type=jnp.float32,
            )
            grown = grown + (both[:, :width] + both[:, width:])
    diag_ref[...] = grown

    for h, send, recv, row in ((0, y_send, y_recv, row_y), (1, x_send, x_recv, row_x)):
        for k in range(cols):
            place = last.at[pl.ds(h * mid, mid), k]
            remote(place, place, send.at[h, k], recv.at[h, k], row, k).wait_recv()
    for copy in started:
        copy.wait_send()


def finish(base, last, column, grown, flags, out_ref, diag_ref):
    rows, cols, share, width = base.shape
    chunk = cols * share // width
    total = grown[...]
    for j in range(rows):
        late = last[j].reshape(cols * share, width)
        value = base[j].reshape(cols * share, width) + late.astype(jnp.float32)
        for q in range(chunk):
            begin = (j * chunk + q) * width
            part = value[q * width:(q + 1) * width] * flags[j * chunk + q, 0:1]
            out_ref[begin:begin + width] = (-part).astype(jnp.bfloat16)
        panel = column[j * cols:(j + 1) * cols].reshape(cols * share, width)
        total = total + lax.dot_general(
            panel, late, (((0,), (0,)), ((), ())), preferred_element_type=jnp.float32
        )
    diag_ref[...] = total


def local(green_blocks, lower_panel, pattern, pivot_inverse):
    rows, cols = lax.axis_size("row"), lax.axis_size("col")
    share, supernodes, width = lower_panel.shape
    blocks = pattern.shape[0]
    mid = rows // 2
    vmem = pl.BlockSpec(memory_space=pltpu.VMEM)
    hbm = pl.BlockSpec(memory_space=pltpu.HBM)
    bf16 = lambda *shape: pltpu.VMEM(shape, jnp.bfloat16)
    dma = lambda *shape: pltpu.SemaphoreType.DMA(shape)
    green = green_blocks.reshape(rows, share, -1)
    buffers = [
        bf16(*green.shape),
        bf16(*lower_panel.shape),
        pltpu.VMEM((share * supernodes, width), jnp.float32),
        pltpu.VMEM((width, width), jnp.float32),
        bf16(cols, supernodes, share, width),
        bf16(2, cols, mid, share, width),
        bf16(2, cols, mid, share, width),
        bf16(cols, rows, share, width),
        bf16(cols, rows, share, width),
        bf16(cols, rows, share, width),
        bf16(cols, rows, share, width),
        bf16(cols, mid, share, width),
        bf16(cols, mid, share, width),
    ]
    held = sum(math.prod(b.shape) * jnp.dtype(b.dtype).itemsize for b in buffers)
    middle = pl.pallas_call(
        functools.partial(exchange, rows, cols),
        out_shape=(
            pltpu.VMEM((rows, cols, share, width), jnp.float32),
            pltpu.VMEM((rows, cols, share, width), jnp.bfloat16),
            pltpu.VMEM((rows * cols, share, width), jnp.bfloat16),
            pltpu.VMEM((width, width), jnp.float32),
            pltpu.VMEM((blocks, 8, width), jnp.float32),
        ),
        in_specs=[hbm] * 4,
        out_specs=(vmem,) * 5,
        scratch_shapes=[pltpu.SMEM(pattern.shape[::-1], pattern.dtype)] + buffers + [
            dma(4), dma(cols), dma(cols), dma(3, cols), dma(3, cols), dma(2), dma(2),
            dma(2, cols), dma(2, cols), dma(2, cols), dma(2, cols), dma(cols), dma(cols),
        ],
        compiler_params=pltpu.CompilerParams(
            collective_id=0, has_side_effects=True, vmem_limit_bytes=held + held // 4 + 4 * 1024 * 1024,
        ),
    )(*(pltpu.with_memory_space_constraint(a, pltpu.HBM) for a in (pattern.T, green, lower_panel, pivot_inverse.reshape(width, width))))
    out, diag = pl.pallas_call(
        finish,
        out_shape=(
            jax.ShapeDtypeStruct((rows * cols * share, width), jnp.bfloat16),
            jax.ShapeDtypeStruct((width, width), jnp.float32),
        ),
        in_specs=[vmem] * 5,
        out_specs=(vmem, vmem),
        compiler_params=pltpu.CompilerParams(vmem_limit_bytes=16 * 1024 * 1024),
    )(*middle)
    return out.reshape(-1, 1, width), diag.reshape(1, width, width)


def solution(mesh):
    placed = (
        P("pole", "col", None, "row"),
        P(("row", "col"), "pole", None),
        P(),
        P(("row", "col"), "pole", None),
    )
    return jax.shard_map(
        local,
        mesh=mesh,
        in_specs=placed,
        out_specs=(P("pole", ("row", "col"), None), P(("row", "col"), "pole", None)),
        check_vma=False,
    )
```

profile of v0, /device:TPU:1, one launch (start us, length us, event | category | flops | bytes accessed | tf_op | source)
XLA Modules:
  0.0 23.9 jit_solution(1458620812054633185)
XLA Ops:
  0.6 22.3 %shard_map.59 = (f32[4,2,192,128]{3,2,1,0:T(8,128)S(1)}, bf16[4,2,192,128]{3,2,1,0:T(8,128)(2,1)S(1)}, bf16[8,192,128]{2,1,0:T(8,128)(2,1)S(1)}, f32[128,128]{1,0:T(8,128)S(1)}, f32[12,8,128]{2,1,0:T(8,128)S(1)}) custom-call(s32[8,12]{1,0:T(8,128)} %bitcast.7, bf16[4,192,384]{2,1,0:T(8,128)(2,1)} %bitcast.5, bf16[192,8,128]{2,1,0:T(8,128)(2,1)} %panel_hbm.1, ...), custom_call_target="tpu_custom_call" | custom-call | tf_op jit(solution)/shard_map/pallas_call | solution.py:241
  22.9 0.9 %shard_map.60 = (bf16[1536,128]{1,0:T(8,128)(2,1)}, f32[128,128]{1,0:T(8,128)}) custom-call(f32[4,2,192,128]{3,2,1,0:T(8,128)S(1)} %get-tuple-element.9.base, bf16[4,2,192,128]{3,2,1,0:T(8,128)(2,1)S(1)} %get-tuple-element.10.last, bf16[8,192,128]{2,1,0:T(8,128)(2,1)S(1)} %get-tuple-element.11.column, f32[128,128]{1,0:T(8,128)S(1)} %get-tuple-element.12.grown, ...), custom_call_target="tpu_custom_call" | custom-call | tf_op jit(solution)/shard_map/pallas_call | solution.py:260
where the time goes:
time: 24 us; the launch traced here: 23.9 us
  Pallas kernels  23.2 us (97%)
  between operations  0.64 us (3%)
    pallas_call x1, Pallas kernels, local(): pl.pallas_call(functools.partial(exchange, rows, cols), out_shape=(pltpu....  22.3 us
    pallas_call x1, Pallas kernels, local(): pl.pallas_call(finish, out_shape=(jax.ShapeDtypeStruct((rows * cols * sha...  0.94 us

commit v1 on v0

v1 whole, which is shorter than its diff:
```python
import functools
import math

import jax
import jax.numpy as jnp
from jax import lax
from jax.experimental import pallas as pl
from jax.experimental.pallas import tpu as pltpu
from jax.sharding import PartitionSpec as P

MESH = pl.DeviceIdType.MESH
PAIR = 2
SPLIT = 2


def exchange(
    rows, cols, pattern_hbm, green_hbm, panel_hbm, pivot_hbm,
    out_ref, diag_ref,
    pattern_ref, green, green_x, panel_ref, wide, pivot_ref, slab, slab_x, column,
    own, to_own, ysum, to_y, far_out, far_in, to_x, xsum,
    load, green_send, green_recv, slab_send, slab_recv, panel_send, panel_recv, share_send, share_recv,
    near_send, near_recv, late_send, late_recv, own_send, own_recv, y_send, y_recv, far_send, far_recv, x_send, x_recv,
):
    r, c = lax.axis_index("row"), lax.axis_index("col")
    me = r * cols + c
    share, supernodes, width = panel_ref.shape
    row_x, row_y, row_far = r + 1 - 2 * (r % 2), (r + 2) % 4, 3 - r
    last = rows - 1
    size = share // SPLIT
    chunks = [(j, s * size) for j in range(last) for s in range(SPLIT)]

    def remote(src, dst, send, recv, row, col):
        return pltpu.make_async_remote_copy(
            src_ref=src, dst_ref=dst, send_sem=send, recv_sem=recv,
            device_id={"row": row, "col": col}, device_id_type=MESH,
        )

    started = []

    def start(copy):
        copy.start()
        started.append(copy)

    def arrived(place, send, recv):
        remote(place, place, send, recv, row_x, c).wait_recv()

    barrier = pltpu.get_barrier_semaphore()
    for row in (row_x, row_y):
        for k in range(cols):
            pl.semaphore_signal(barrier, 1, device_id={"row": row, "col": k}, device_id_type=MESH)
    for step in range(1, cols):
        pl.semaphore_signal(barrier, 1, device_id={"row": r, "col": (c + step) % cols}, device_id_type=MESH)
    loads = [
        pltpu.make_async_copy(panel_hbm, panel_ref, load.at[0]),
        pltpu.make_async_copy(pattern_hbm, pattern_ref, load.at[3]),
        pltpu.make_async_copy(green_hbm, green, load.at[1]),
        pltpu.make_async_copy(pivot_hbm, pivot_ref, load.at[2]),
    ]
    for copy in loads:
        copy.start()
    pl.semaphore_wait(barrier, 3 * cols - 1)

    def send_green(i):
        j, a = chunks[i]
        start(remote(
            green_hbm.at[j, pl.ds(a, size)], green_x.at[j, pl.ds(a, size)],
            green_send.at[i], green_recv.at[i], row_x, c,
        ))

    send_green(0)

    loads[0].wait()
    loads[1].wait()
    wide[...] = panel_ref[...].astype(jnp.float32).reshape(share * supernodes, width)
    piece = math.gcd(share, width)
    for k in range(supernodes):
        value = wide[pl.ds(k, share, stride=supernodes), :]
        parts = []
        for q in range(share // piece):
            flag = pattern_ref[k, (me * share + q * piece) // width].astype(jnp.float32)
            parts.append(value[q * piece:(q + 1) * piece] * flag)
        slab[c, k] = jnp.concatenate(parts, axis=0).astype(jnp.bfloat16)

    def group(row):
        return pl.ds(row * cols, cols)

    for g, row in ((1, row_far), (0, row_x)):
        start(remote(
            slab.at[c, group(row)], slab_x.at[c, g], panel_send.at[g], panel_recv.at[g], row_x, c,
        ))
    for k in range(cols):
        start(remote(
            slab.at[c, row_y * cols + k], column.at[me], near_send.at[k], near_recv.at[c], row_y, k,
        ))
    for step in range(1, cols):
        k = (c + step) % cols
        start(remote(slab.at[c], slab.at[c], slab_send.at[k], slab_recv.at[c], r, k))
    for i in range(1, len(chunks)):
        send_green(i)
    loads[2].wait()
    for step in range(1, cols):
        k = (c + step) % cols
        arrived(slab.at[k], slab_send.at[k], slab_recv.at[k])

    def pairs(body):
        if cols == PAIR:
            body(0)
        else:
            lax.fori_loop(0, cols // PAIR, lambda i, z: (body(i * PAIR), z)[1], 0)

    def stack(pick, k):
        return jnp.concatenate(
            [jnp.concatenate([pick(s, k + p) for s in range(cols)], axis=0) for p in range(PAIR)], axis=1
        )

    def alone(put, row):
        def body(k):
            rhs = stack(lambda s, q: slab[s, row * cols + q], k)
            value = jnp.dot(green[last], rhs, preferred_element_type=jnp.float32).astype(jnp.bfloat16)
            for p in range(PAIR):
                put(k + p, value[:, p * width:(p + 1) * width])

        pairs(body)

    def both(put, i, g, row):
        j, a = chunks[i]

        def body(k):
            rhs = jnp.concatenate(
                [stack(lambda s, q: slab[s, row * cols + q], k), stack(lambda s, q: slab_x[s, g, q], k)], axis=0
            )
            lhs = jnp.concatenate([green[j, a:a + size], green_x[j, a:a + size]], axis=1)
            value = jnp.dot(lhs, rhs, preferred_element_type=jnp.float32).astype(jnp.bfloat16)
            for p in range(PAIR):
                put(k + p, value[:, p * width:(p + 1) * width])

        pairs(body)

    def into(buffer, *at):
        def put(k, value):
            buffer[(k,) + at] = value
        return put

    alone(into(far_out), row_far)
    start(remote(far_out, far_in, far_send.at[0], far_recv.at[0], row_y, c))
    alone(into(to_y, last), row_y)
    count = len(chunks)
    for k in range(cols):
        start(remote(to_y.at[k, last], ysum.at[c, last], y_send.at[count, k], y_recv.at[count, c], row_y, k))
    alone(into(to_own, last), r)
    for step in range(1, cols):
        k = (c + step) % cols
        start(remote(to_own.at[k, last], own.at[c, last], own_send.at[count, k], own_recv.at[count, c], r, k))
    own[c, last] = to_own[c, last]
    alone(into(to_x), row_x)

    for g in (1, 0):
        arrived(slab_x.at[c, g], panel_send.at[g], panel_recv.at[g])
        for step in range(1, cols):
            k = (c + step) % cols
            start(remote(slab_x.at[c, g], slab_x.at[c, g], share_send.at[g, k], share_recv.at[g, c], r, k))
        if g == 1:
            for k in range(cols):
                start(remote(
                    slab_x.at[c, 1, k], column.at[row_x * cols + c], late_send.at[k], late_recv.at[c], row_y, k,
                ))

    def shared(g):
        for step in range(1, cols):
            k = (c + step) % cols
            arrived(slab_x.at[k, g], share_send.at[g, k], share_recv.at[g, k])

    def send_sum(i):
        j, a = chunks[i]
        arrived(green_x.at[j, pl.ds(a, size)], green_send.at[i], green_recv.at[i])
        both(into(to_y, j, slice(a, a + size)), i, 1, row_y)
        for k in range(cols):
            start(remote(
                to_y.at[k, j, pl.ds(a, size)], ysum.at[c, j, pl.ds(a, size)],
                y_send.at[i, k], y_recv.at[i, c], row_y, k,
            ))

    def keep_sum(i):
        j, a = chunks[i]
        both(into(to_own, j, slice(a, a + size)), i, 0, r)
        for step in range(1, cols):
            k = (c + step) % cols
            start(remote(
                to_own.at[k, j, pl.ds(a, size)], own.at[c, j, pl.ds(a, size)],
                own_send.at[i, k], own_recv.at[i, c], r, k,
            ))
        own[c, j, a:a + size] = to_own[c, j, a:a + size]

    def finish(i, j, a, n, late):
        for step in range(1, cols):
            k = (c + step) % cols
            arrived(own.at[k, j, pl.ds(a, n)], own_send.at[i, k], own_recv.at[i, k])
        for k in range(cols):
            arrived(ysum.at[k, j, pl.ds(a, n)], y_send.at[i, k], y_recv.at[i, k])
        cuts = sorted({a, a + n} | set(range(-(-a // piece) * piece, a + n, piece)))
        held = []
        for k in range(cols):
            begin = (j * cols + k) * share
            terms = [own[k, j, a:a + n], ysum[k, j, a:a + n]] + ([late[k, a:a + n]] if late is not None else [])
            held.append(jnp.concatenate(terms, axis=1))
            value = sum(term.astype(jnp.float32) for term in terms)
            for low, high in zip(cuts[:-1], cuts[1:]):
                flag = pattern_ref[me, (begin + low) // width].astype(jnp.float32)
                out_ref[begin + low:begin + high] = (-(value[low - a:high - a] * flag)).astype(jnp.bfloat16)
        lhs = jnp.concatenate([column[j * cols + k, a:a + n] for k in range(cols)], axis=0)
        grown = lax.dot_general(
            lhs, jnp.concatenate(held, axis=0), (((0,), (0,)), ((), ())), preferred_element_type=jnp.float32,
        )
        total = diag_ref[...]
        for t in range(grown.shape[1] // width):
            total = total + grown[:, t * width:(t + 1) * width]
        diag_ref[...] = total

    shared(1)
    send_sum(0)
    arrived(far_in, far_send.at[0], far_recv.at[0])
    to_x[...] = (to_x[...].astype(jnp.float32) + far_in[...].astype(jnp.float32)).astype(jnp.bfloat16)
    for k in range(cols):
        start(remote(to_x.at[k], xsum.at[c], x_send.at[k], x_recv.at[c], row_x, k))
    shared(0)
    keep_sum(0)
    send_sum(1)
    keep_sum(1)
    for s in range(cols):
        column[r * cols + s] = slab[s, me]
        column[row_x * cols + s] = slab_x[s, 0, c]
    loads[3].wait()
    diag_ref[...] = pivot_ref[...]
    for k in range(cols):
        place = column.at[row_y * cols + k]
        arrived(place, near_send.at[k], near_recv.at[k])
    for i in range(2, count):
        send_sum(i)
        keep_sum(i)
        if i == 2:
            for k in range(cols):
                place = column.at[row_far * cols + k]
                arrived(place, late_send.at[k], late_recv.at[k])
        if i >= 3:
            finish(i - 3, *chunks[i - 3], size, None)
    for i in range(count - 3, count - 1):
        finish(i, *chunks[i], size, None)
    for k in range(cols):
        arrived(xsum.at[k], x_send.at[k], x_recv.at[k])
    finish(count, last, 0, share, xsum)
    finish(count - 1, *chunks[count - 1], size, None)
    for copy in started:
        copy.wait_send()


def store(made, grown, out_ref, diag_ref, sems):
    copies = [pltpu.make_async_copy(made, out_ref, sems.at[0]), pltpu.make_async_copy(grown, diag_ref, sems.at[1])]
    for copy in copies:
        copy.start()
    for copy in copies:
        copy.wait()


def local(green_blocks, lower_panel, pattern, pivot_inverse):
    rows, cols = lax.axis_size("row"), lax.axis_size("col")
    share, supernodes, width = lower_panel.shape
    vmem = pl.BlockSpec(memory_space=pltpu.VMEM)
    hbm = pl.BlockSpec(memory_space=pltpu.HBM)
    bf16 = lambda *shape: pltpu.VMEM(shape, jnp.bfloat16)
    dma = lambda *shape: pltpu.SemaphoreType.DMA(shape)
    green = green_blocks.reshape(rows, share, -1)
    depth = green.shape[2]
    count = (rows - 1) * SPLIT
    buffers = [
        bf16(*green.shape),
        bf16(rows - 1, share, depth),
        bf16(*lower_panel.shape),
        pltpu.VMEM((share * supernodes, width), jnp.float32),
        pltpu.VMEM((width, width), jnp.float32),
        bf16(cols, supernodes, share, width),
        bf16(cols, 2, cols, share, width),
        bf16(rows * cols, share, width),
        bf16(cols, rows, share, width),
        bf16(cols, rows, share, width),
        bf16(cols, rows, share, width),
        bf16(cols, rows, share, width),
        bf16(cols, share, width),
        bf16(cols, share, width),
        bf16(cols, share, width),
        bf16(cols, share, width),
    ]
    held = sum(math.prod(b.shape) * jnp.dtype(b.dtype).itemsize for b in buffers)
    middle = pl.pallas_call(
        functools.partial(exchange, rows, cols),
        out_shape=(
            pltpu.VMEM((rows * cols * share, width), jnp.bfloat16),
            pltpu.VMEM((width, width), jnp.float32),
        ),
        in_specs=[hbm] * 4,
        out_specs=(vmem,) * 2,
        scratch_shapes=[pltpu.SMEM(pattern.shape[::-1], pattern.dtype)] + buffers + [
            dma(4), dma(count), dma(count), dma(cols), dma(cols), dma(2), dma(2), dma(2, cols), dma(2, cols),
            dma(cols), dma(cols), dma(cols), dma(cols), dma(count + 1, cols), dma(count + 1, cols),
            dma(count + 1, cols), dma(count + 1, cols), dma(1), dma(1), dma(cols), dma(cols),
        ],
        compiler_params=pltpu.CompilerParams(
            collective_id=0, has_side_effects=True, vmem_limit_bytes=held + held // 4 + 4 * 1024 * 1024,
        ),
    )(*(pltpu.with_memory_space_constraint(a, pltpu.HBM) for a in (pattern.T, green, lower_panel, pivot_inverse.reshape(width, width))))
    out, diag = pl.pallas_call(
        store,
        out_shape=(
            jax.ShapeDtypeStruct((rows * cols * share, width), jnp.bfloat16),
            jax.ShapeDtypeStruct((width, width), jnp.float32),
        ),
        in_specs=[vmem] * 2,
        out_specs=(hbm, hbm),
        scratch_shapes=[dma(2)],
        compiler_params=pltpu.CompilerParams(vmem_limit_bytes=16 * 1024 * 1024),
    )(*middle)
    return out.reshape(-1, 1, width), diag.reshape(1, width, width)


def solution(mesh):
    placed = (
        P("pole", "col", None, "row"),
        P(("row", "col"), "pole", None),
        P(),
        P(("row", "col"), "pole", None),
    )
    return jax.shard_map(
        local,
        mesh=mesh,
        in_specs=placed,
        out_specs=(P("pole", ("row", "col"), None), P(("row", "col"), "pole", None)),
        check_vma=False,
    )
```

time: 24 us -> 25.3 us (1.054)
  the two profiles are of different devices: /device:TPU:1 before, /device:TPU:0 now
where the time goes in v1:
time: 25.3 us; the launch traced here: 25.1 us
  Pallas kernels  24.5 us (97%)
  between operations  0.64 us (3%)
    pallas_call x1, Pallas kernels, local(): pl.pallas_call(functools.partial(exchange, rows, cols), out_shape=(pltpu....  23.7 us
    pallas_call x1, Pallas kernels, local(): pl.pallas_call(store, out_shape=(jax.ShapeDtypeStruct((rows * cols * shar...  0.78 us

profile of v1, /device:TPU:0, one launch (start us, length us, event | category | flops | bytes accessed | tf_op | source)
XLA Modules:
  0.0 25.1 jit_solution(1478355810063196410)
XLA Ops:
  0.6 23.7 %shard_map.59 = (bf16[1536,128]{1,0:T(8,128)(2,1)S(1)}, f32[128,128]{1,0:T(8,128)S(1)}) custom-call(s32[8,12]{1,0:T(8,128)} %bitcast.7, bf16[4,192,384]{2,1,0:T(8,128)(2,1)} %bitcast.5, bf16[192,8,128]{2,1,0:T(8,128)(2,1)} %panel_hbm.1, f32[128,128]{1,0:T(8,128)} %bitcast.6), custom_call_target="tpu_custom_call" | custom-call | tf_op jit(solution)/shard_map/pallas_call | solution.py:293
  24.3 0.8 %shard_map.60 = (bf16[1536,128]{1,0:T(8,128)(2,1)}, f32[128,128]{1,0:T(8,128)}) custom-call(bf16[1536,128]{1,0:T(8,128)(2,1)S(1)} %get-tuple-element.6.made, f32[128,128]{1,0:T(8,128)S(1)} %get-tuple-element.7.grown), custom_call_target="tpu_custom_call" | custom-call | tf_op jit(solution)/shard_map/pallas_call | solution.py:310

commit v2 on v1

v2 whole, which is shorter than its diff:
```python
import functools
import math

import jax
import jax.numpy as jnp
from jax import lax
from jax.experimental import pallas as pl
from jax.experimental.pallas import tpu as pltpu
from jax.sharding import PartitionSpec as P

MESH = pl.DeviceIdType.MESH
PAIR = 2
STEPS = (7, 7, 6, 5, 4, 3)


def plan(total):
    unit = total // 3 * 2 // sum(STEPS) // 16 * 16
    ends = [0]
    for step in STEPS:
        ends.append(ends[-1] + step * unit)
    return list(zip(ends[:-1], ends[1:]))


def exchange(
    rows, cols, pattern_hbm, green_hbm, panel_hbm, pivot_hbm,
    out_ref, diag_ref,
    pattern_ref, green, green_x, panel_ref, wide, pivot_ref, slab, slab_x, column,
    own, to_own, ysum, to_y, far_out, far_in, to_x, xsum,
    load, green_recv, y_recv, own_recv, panel_recv, share_recv, one_recv, sent,
):
    r, c = lax.axis_index("row"), lax.axis_index("col")
    me = r * cols + c
    share, supernodes, width = panel_ref.shape
    row_x, row_y, row_far = r + 1 - 2 * (r % 2), (r + 2) % 4, 3 - r
    total = rows * share
    chunks = plan(total)
    count = len(chunks)
    split = chunks[-1][1]
    tail = slice(split, total)
    slab_recv, near_recv, late_recv, far_recv, x_recv = (one_recv.at[i] for i in range(5))
    (
        green_sent, panel_sent, slab_sent, share_sent, near_sent, late_sent, own_sent, y_sent, far_sent, x_sent
    ) = (sent.at[i] for i in range(10))

    def start(src, dst, send, recv, row, col):
        pltpu.make_async_remote_copy(
            src_ref=src, dst_ref=dst, send_sem=send, recv_sem=recv,
            device_id={"row": row, "col": col}, device_id_type=MESH,
        ).start()

    def arrived(place, recv):
        pltpu.make_async_copy(place, place, recv).wait()

    others = [(c + step) % cols for step in range(1, cols)]
    barrier = pltpu.get_barrier_semaphore()
    for row in (row_x, row_y):
        for k in range(cols):
            pl.semaphore_signal(barrier, 1, device_id={"row": row, "col": k}, device_id_type=MESH)
    for k in others:
        pl.semaphore_signal(barrier, 1, device_id={"row": r, "col": k}, device_id_type=MESH)
    loads = [
        pltpu.make_async_copy(panel_hbm, panel_ref, load.at[0]),
        pltpu.make_async_copy(pattern_hbm, pattern_ref, load.at[3]),
        pltpu.make_async_copy(green_hbm, green, load.at[1]),
        pltpu.make_async_copy(pivot_hbm, pivot_ref, load.at[2]),
    ]
    for copy in loads:
        copy.start()

    loads[0].wait()
    loads[1].wait()
    wide[...] = panel_ref[...].astype(jnp.float32).reshape(share * supernodes, width)
    piece = math.gcd(share, width)
    for k in range(supernodes):
        value = wide[pl.ds(k, share, stride=supernodes), :]
        parts = []
        for q in range(share // piece):
            flag = pattern_ref[k, (me * share + q * piece) // width].astype(jnp.float32)
            parts.append(value[q * piece:(q + 1) * piece] * flag)
        slab[c, k] = jnp.concatenate(parts, axis=0).astype(jnp.bfloat16)
    loads[2].wait()
    loads[3].wait()
    diag_ref[...] = pivot_ref[...]
    pl.semaphore_wait(barrier, 3 * cols - 1)

    def group(row):
        return pl.ds(row * cols, cols)

    for g, row in ((1, row_far), (0, row_x)):
        start(slab.at[c, group(row)], slab_x.at[c, g], panel_sent, panel_recv.at[g], row_x, c)
    for k in others:
        start(slab.at[c], slab.at[c], slab_sent, slab_recv, r, k)
    for k in range(cols):
        start(slab.at[c, row_y * cols + k], column.at[me], near_sent, near_recv, row_y, k)
    for i, (low, high) in enumerate(chunks):
        span = pl.ds(low, high - low)
        start(green.at[span], green_x.at[span], green_sent, green_recv.at[i], row_x, c)

    def pairs(body):
        if cols == PAIR:
            body(0)
        else:
            lax.fori_loop(0, cols // PAIR, lambda i, z: (body(i * PAIR), z)[1], 0)

    def stack(pick, k):
        return jnp.concatenate(
            [jnp.concatenate([pick(s, k + p) for s in range(cols)], axis=0) for p in range(PAIR)], axis=1
        )

    def product(buffer, at, lhs, rhs):
        def body(k):
            value = jnp.dot(lhs(), rhs(k), preferred_element_type=jnp.float32).astype(jnp.bfloat16)
            for p in range(PAIR):
                buffer[k + p, at] = value[:, p * width:(p + 1) * width]

        pairs(body)

    def alone(buffer, at, row):
        product(buffer, at, lambda: green[tail], lambda k: stack(lambda s, q: slab[s, row * cols + q], k))

    def joint(buffer, i, g, row):
        at = slice(*chunks[i])
        product(
            buffer, at,
            lambda: jnp.concatenate([green[at], green_x[at]], axis=1),
            lambda k: jnp.concatenate(
                [stack(lambda s, q: slab[s, row * cols + q], k), stack(lambda s, q: slab_x[s, g, q], k)], axis=0
            ),
        )

    rest = pl.ds(split, total - split)
    arrived(slab.at[pl.ds(0, cols - 1)], slab_recv)
    alone(far_out, slice(None), row_far)
    start(far_out, far_in, far_sent, far_recv, row_y, c)
    alone(to_y, tail, row_y)
    for k in range(cols):
        start(to_y.at[k, rest], ysum.at[c, rest], y_sent, y_recv.at[count], row_y, k)
    alone(to_own, tail, r)
    for k in others:
        start(to_own.at[k, rest], own.at[c, rest], own_sent, own_recv.at[count], r, k)
    own[c, tail] = to_own[c, tail]
    alone(to_x, slice(None), row_x)

    def pass_on(g):
        arrived(slab_x.at[c, g], panel_recv.at[g])
        for k in others:
            start(slab_x.at[c, g], slab_x.at[c, g], share_sent, share_recv.at[g], r, k)

    def shared(g):
        arrived(slab_x.at[pl.ds(0, cols - 1), g], share_recv.at[g])

    pass_on(1)
    for k in range(cols):
        start(slab_x.at[c, 1, k], column.at[row_x * cols + c], late_sent, late_recv, row_y, k)
    pass_on(0)
    arrived(far_in, far_recv)
    to_x[...] = (to_x[...].astype(jnp.float32) + far_in[...].astype(jnp.float32)).astype(jnp.bfloat16)
    for k in range(cols):
        start(to_x.at[k], xsum.at[c], x_sent, x_recv, row_x, k)

    def send_sum(i):
        low, high = chunks[i]
        span = pl.ds(low, high - low)
        arrived(green_x.at[span], green_recv.at[i])
        joint(to_y, i, 1, row_y)
        for k in range(cols):
            start(to_y.at[k, span], ysum.at[c, span], y_sent, y_recv.at[i], row_y, k)

    def keep_sum(i):
        low, high = chunks[i]
        span = pl.ds(low, high - low)
        joint(to_own, i, 0, r)
        for k in others:
            start(to_own.at[k, span], own.at[c, span], own_sent, own_recv.at[i], r, k)
        own[c, low:high] = to_own[c, low:high]

    def finish(i, low, high, late):
        span = pl.ds(low, high - low)
        arrived(own.at[pl.ds(0, cols - 1), span], own_recv.at[i])
        arrived(ysum.at[:, span], y_recv.at[i])
        lhs, rhs = [], []
        for k in range(cols):
            terms = [own[k, low:high], ysum[k, low:high]] + ([late[k]] if late is not None else [])
            rhs.append(jnp.concatenate(terms, axis=1))
            value = sum(term.astype(jnp.float32) for term in terms)
            cuts = sorted({low, high} | set(range(-(-low // piece) * piece, high, piece)))
            for first, end in zip(cuts[:-1], cuts[1:]):
                begin = (first // share * cols + k) * share + first % share
                flag = pattern_ref[me, begin // width].astype(jnp.float32)
                out_ref[begin:begin + end - first] = (-(value[first - low:end - low] * flag)).astype(jnp.bfloat16)
            cuts = sorted({low, high} | set(range(-(-low // share) * share, high, share)))
            for first, end in zip(cuts[:-1], cuts[1:]):
                a = first % share
                lhs.append(column[first // share * cols + k, a:a + end - first])
        grown = lax.dot_general(
            jnp.concatenate(lhs, axis=0), jnp.concatenate(rhs, axis=0),
            (((0,), (0,)), ((), ())), preferred_element_type=jnp.float32,
        )
        value = diag_ref[...]
        for t in range(grown.shape[1] // width):
            value = value + grown[:, t * width:(t + 1) * width]
        diag_ref[...] = value

    shared(1)
    send_sum(0)
    shared(0)
    keep_sum(0)
    for s in range(cols):
        column[r * cols + s] = slab[s, me]
        column[row_x * cols + s] = slab_x[s, 0, c]
    send_sum(1)
    keep_sum(1)
    send_sum(2)
    keep_sum(2)
    arrived(column.at[group(row_y)], near_recv)
    arrived(column.at[group(row_far)], late_recv)
    for i in range(3, count):
        send_sum(i)
        keep_sum(i)
        finish(i - 3, *chunks[i - 3], None)
    for i in range(count - 3, count - 1):
        finish(i, *chunks[i], None)
    arrived(xsum, x_recv)
    finish(count, split, total, xsum)
    finish(count - 1, *chunks[count - 1], None)
    for place, sem in (
        (green_x, green_sent), (slab_x.at[0], panel_sent), (slab.at[pl.ds(0, cols - 1)], slab_sent),
        (slab_x.at[pl.ds(0, cols - 1)], share_sent), (column.at[pl.ds(0, cols)], near_sent),
        (column.at[pl.ds(0, cols)], late_sent), (own.at[pl.ds(0, cols - 1)], own_sent), (ysum, y_sent),
        (far_out, far_sent), (to_x, x_sent),
    ):
        arrived(place, sem)


def store(made, grown, out_ref, diag_ref, sems):
    copies = [pltpu.make_async_copy(made, out_ref, sems.at[0]), pltpu.make_async_copy(grown, diag_ref, sems.at[1])]
    for copy in copies:
        copy.start()
    for copy in copies:
        copy.wait()


def local(green_blocks, lower_panel, pattern, pivot_inverse):
    rows, cols = lax.axis_size("row"), lax.axis_size("col")
    share, supernodes, width = lower_panel.shape
    vmem = pl.BlockSpec(memory_space=pltpu.VMEM)
    hbm = pl.BlockSpec(memory_space=pltpu.HBM)
    bf16 = lambda *shape: pltpu.VMEM(shape, jnp.bfloat16)
    dma = lambda *shape: pltpu.SemaphoreType.DMA(shape)
    total = rows * share
    green = green_blocks.reshape(total, -1)
    depth = green.shape[1]
    chunks = plan(total)
    count, split = len(chunks), chunks[-1][1]
    buffers = [
        bf16(total, depth),
        bf16(split, depth),
        bf16(*lower_panel.shape),
        pltpu.VMEM((share * supernodes, width), jnp.float32),
        pltpu.VMEM((width, width), jnp.float32),
        bf16(cols, supernodes, share, width),
        bf16(cols, 2, cols, share, width),
        bf16(rows * cols, share, width),
        bf16(cols, total, width),
        bf16(cols, total, width),
        bf16(cols, total, width),
        bf16(cols, total, width),
        bf16(cols, total - split, width),
        bf16(cols, total - split, width),
        bf16(cols, total - split, width),
        bf16(cols, total - split, width),
    ]
    held = sum(math.prod(b.shape) * jnp.dtype(b.dtype).itemsize for b in buffers)
    middle = pl.pallas_call(
        functools.partial(exchange, rows, cols),
        out_shape=(
            pltpu.VMEM((cols * total, width), jnp.bfloat16),
            pltpu.VMEM((width, width), jnp.float32),
        ),
        in_specs=[hbm] * 4,
        out_specs=(vmem,) * 2,
        scratch_shapes=[pltpu.SMEM(pattern.shape[::-1], pattern.dtype)] + buffers + [
            dma(4), dma(count), dma(count + 1), dma(count + 1), dma(2), dma(2), dma(5), dma(10),
        ],
        compiler_params=pltpu.CompilerParams(
            collective_id=0, has_side_effects=True, vmem_limit_bytes=held + held // 4 + 4 * 1024 * 1024,
        ),
    )(*(pltpu.with_memory_space_constraint(a, pltpu.HBM) for a in (pattern.T, green, lower_panel, pivot_inverse.reshape(width, width))))
    out, diag = pl.pallas_call(
        store,
        out_shape=(
            jax.ShapeDtypeStruct((cols * total, width), jnp.bfloat16),
            jax.ShapeDtypeStruct((width, width), jnp.float32),
        ),
        in_specs=[vmem] * 2,
        out_specs=(hbm, hbm),
        scratch_shapes=[dma(2)],
        compiler_params=pltpu.CompilerParams(vmem_limit_bytes=16 * 1024 * 1024),
    )(*middle)
    return out.reshape(-1, 1, width), diag.reshape(1, width, width)


def solution(mesh):
    placed = (
        P("pole", "col", None, "row"),
        P(("row", "col"), "pole", None),
        P(),
        P(("row", "col"), "pole", None),
    )
    return jax.shard_map(
        local,
        mesh=mesh,
        in_specs=placed,
        out_specs=(P("pole", ("row", "col"), None), P(("row", "col"), "pole", None)),
        check_vma=False,
    )
```

time: 25.3 us -> 24 us (0.949)
  Pallas kernels: 24.5 us -> 23.2 us
    pallas_call x1, Pallas kernels: 23.7 us -> 22.4 us  [local(): pl.pallas_call(functools.partial(exchange, rows, cols), out_shape=(pltpu....]
where the time goes in v2:
time: 24 us; the launch traced here: 23.8 us
  Pallas kernels  23.2 us (97%)
  between operations  0.64 us (3%)
    pallas_call x1, Pallas kernels, local(): pl.pallas_call(functools.partial(exchange, rows, cols), out_shape=(pltpu....  22.4 us
    pallas_call x1, Pallas kernels, local(): pl.pallas_call(store, out_shape=(jax.ShapeDtypeStruct((cols * total, widt...  0.78 us

profile of v2, /device:TPU:0, one launch (start us, length us, event | category | flops | bytes accessed | tf_op | source)
XLA Modules:
  0.0 23.8 jit_solution(11721506314205777652)
XLA Ops:
  0.6 22.4 %shard_map.59 = (bf16[1536,128]{1,0:T(8,128)(2,1)S(1)}, f32[128,128]{1,0:T(8,128)S(1)}) custom-call(s32[8,12]{1,0:T(8,128)} %bitcast.7, bf16[768,384]{1,0:T(8,128)(2,1)} %bitcast.5, bf16[192,8,128]{2,1,0:T(8,128)(2,1)} %panel_hbm.1, f32[128,128]{1,0:T(8,128)} %bitcast.6), custom_call_target="tpu_custom_call" | custom-call | tf_op jit(solution)/shard_map/pallas_call | solution.py:274
  23.0 0.8 %shard_map.60 = (bf16[1536,128]{1,0:T(8,128)(2,1)}, f32[128,128]{1,0:T(8,128)}) custom-call(bf16[1536,128]{1,0:T(8,128)(2,1)S(1)} %get-tuple-element.6.made, f32[128,128]{1,0:T(8,128)S(1)} %get-tuple-element.7.grown), custom_call_target="tpu_custom_call" | custom-call | tf_op jit(solution)/shard_map/pallas_call | solution.py:289

commit v3 on v2

--- a/solution.py
+++ b/solution.py
@@ -10,11 +10,12 @@
 
 MESH = pl.DeviceIdType.MESH
 PAIR = 2
-STEPS = (7, 7, 6, 5, 4, 3)
+LAG = 2
+STEPS = (10, 9, 8, 3)
 
 
 def plan(total):
-    unit = total // 3 * 2 // sum(STEPS) // 16 * 16
+    unit = total // 48
     ends = [0]
     for step in STEPS:
         ends.append(ends[-1] + step * unit)
@@ -201,6 +202,10 @@
             value = value + grown[:, t * width:(t + 1) * width]
         diag_ref[...] = value
 
+    def columns():
+        arrived(column.at[group(row_y)], near_recv)
+        arrived(column.at[group(row_far)], late_recv)
+
     shared(1)
     send_sum(0)
     shared(0)
@@ -208,17 +213,16 @@
     for s in range(cols):
         column[r * cols + s] = slab[s, me]
         column[row_x * cols + s] = slab_x[s, 0, c]
-    send_sum(1)
-    keep_sum(1)
-    send_sum(2)
-    keep_sum(2)
-    arrived(column.at[group(row_y)], near_recv)
-    arrived(column.at[group(row_far)], late_recv)
-    for i in range(3, count):
+    for i in range(1, count):
         send_sum(i)
         keep_sum(i)
-        finish(i - 3, *chunks[i - 3], None)
-    for i in range(count - 3, count - 1):
+        if i >= LAG:
+            if i == LAG:
+                columns()
+            finish(i - LAG, *chunks[i - LAG], None)
+    if count <= LAG:
+        columns()
+    for i in range(max(count - LAG, 0), count - 1):
         finish(i, *chunks[i], None)
     arrived(xsum, x_recv)
     finish(count, split, total, xsum)

time: 24 us -> 23.4 us (0.975)
  Pallas kernels: 23.2 us -> 22.6 us
    pallas_call x1, Pallas kernels: 22.4 us -> 21.8 us  [local(): pl.pallas_call(functools.partial(exchange, rows, cols), out_shape=(pltpu....]
where the time goes in v3:
time: 23.4 us; the launch traced here: 23.2 us
  Pallas kernels  22.6 us (97%)
  between operations  0.64 us (3%)
    pallas_call x1, Pallas kernels, local(): pl.pallas_call(functools.partial(exchange, rows, cols), out_shape=(pltpu....  21.8 us
    pallas_call x1, Pallas kernels, local(): pl.pallas_call(store, out_shape=(jax.ShapeDtypeStruct((cols * total, widt...  0.78 us

profile of v3, /device:TPU:0, one launch (start us, length us, event | category | flops | bytes accessed | tf_op | source)
XLA Modules:
  0.0 23.2 jit_solution(16227107969415816366)
XLA Ops:
  0.6 21.8 %shard_map.59 = (bf16[1536,128]{1,0:T(8,128)(2,1)S(1)}, f32[128,128]{1,0:T(8,128)S(1)}) custom-call(s32[8,12]{1,0:T(8,128)} %bitcast.7, bf16[768,384]{1,0:T(8,128)(2,1)} %bitcast.5, bf16[192,8,128]{2,1,0:T(8,128)(2,1)} %panel_hbm.1, f32[128,128]{1,0:T(8,128)} %bitcast.6), custom_call_target="tpu_custom_call" | custom-call | tf_op jit(solution)/shard_map/pallas_call | solution.py:278
  22.5 0.8 %shard_map.60 = (bf16[1536,128]{1,0:T(8,128)(2,1)}, f32[128,128]{1,0:T(8,128)}) custom-call(bf16[1536,128]{1,0:T(8,128)(2,1)S(1)} %get-tuple-element.6.made, f32[128,128]{1,0:T(8,128)S(1)} %get-tuple-element.7.grown), custom_call_target="tpu_custom_call" | custom-call | tf_op jit(solution)/shard_map/pallas_call | solution.py:293

commit v4 on v3

--- a/solution.py
+++ b/solution.py
@@ -11,7 +11,7 @@
 MESH = pl.DeviceIdType.MESH
 PAIR = 2
 LAG = 2
-STEPS = (10, 9, 8, 3)
+STEPS = (10, 10, 7, 3)
 
 
 def plan(total):
@@ -222,10 +222,11 @@
             finish(i - LAG, *chunks[i - LAG], None)
     if count <= LAG:
         columns()
-    for i in range(max(count - LAG, 0), count - 1):
+    for i in range(max(count - LAG, 0), count - 2):
         finish(i, *chunks[i], None)
     arrived(xsum, x_recv)
     finish(count, split, total, xsum)
+    finish(count - 2, *chunks[count - 2], None)
     finish(count - 1, *chunks[count - 1], None)
     for place, sem in (
         (green_x, green_sent), (slab_x.at[0], panel_sent), (slab.at[pl.ds(0, cols - 1)], slab_sent),

time: 23.4 us -> 23.4 us (level)
  no operation moved by 1% of the time
where the time goes in v4:
time: 23.4 us; the launch traced here: 23.2 us
  Pallas kernels  22.6 us (97%)
  between operations  0.64 us (3%)
    pallas_call x1, Pallas kernels, local(): pl.pallas_call(functools.partial(exchange, rows, cols), out_shape=(pltpu....  21.8 us
    pallas_call x1, Pallas kernels, local(): pl.pallas_call(store, out_shape=(jax.ShapeDtypeStruct((cols * total, widt...  0.78 us

profile of v4, /device:TPU:0, one launch (start us, length us, event | category | flops | bytes accessed | tf_op | source)
XLA Modules:
  0.0 23.2 jit_solution(10592386202717002858)
XLA Ops:
  0.6 21.8 %shard_map.59 = (bf16[1536,128]{1,0:T(8,128)(2,1)S(1)}, f32[128,128]{1,0:T(8,128)S(1)}) custom-call(s32[8,12]{1,0:T(8,128)} %bitcast.7, bf16[768,384]{1,0:T(8,128)(2,1)} %bitcast.5, bf16[192,8,128]{2,1,0:T(8,128)(2,1)} %panel_hbm.1, f32[128,128]{1,0:T(8,128)} %bitcast.6), custom_call_target="tpu_custom_call" | custom-call | tf_op jit(solution)/shard_map/pallas_call | solution.py:279
  22.5 0.8 %shard_map.60 = (bf16[1536,128]{1,0:T(8,128)(2,1)}, f32[128,128]{1,0:T(8,128)}) custom-call(bf16[1536,128]{1,0:T(8,128)(2,1)S(1)} %get-tuple-element.6.made, f32[128,128]{1,0:T(8,128)S(1)} %get-tuple-element.7.grown), custom_call_target="tpu_custom_call" | custom-call | tf_op jit(solution)/shard_map/pallas_call | solution.py:294

commit v5 on v4

--- a/solution.py
+++ b/solution.py
@@ -11,6 +11,7 @@
 MESH = pl.DeviceIdType.MESH
 PAIR = 2
 LAG = 2
+AHEAD = 1
 STEPS = (10, 10, 7, 3)
 
 
@@ -87,15 +88,23 @@
     def group(row):
         return pl.ds(row * cols, cols)
 
-    for g, row in ((1, row_far), (0, row_x)):
+    def send_panel(g, row):
         start(slab.at[c, group(row)], slab_x.at[c, g], panel_sent, panel_recv.at[g], row_x, c)
+
+    def send_green(i):
+        low, high = chunks[i]
+        span = pl.ds(low, high - low)
+        start(green.at[span], green_x.at[span], green_sent, green_recv.at[i], row_x, c)
+
+    send_panel(1, row_far)
     for k in others:
         start(slab.at[c], slab.at[c], slab_sent, slab_recv, r, k)
     for k in range(cols):
         start(slab.at[c, row_y * cols + k], column.at[me], near_sent, near_recv, row_y, k)
-    for i, (low, high) in enumerate(chunks):
-        span = pl.ds(low, high - low)
-        start(green.at[span], green_x.at[span], green_sent, green_recv.at[i], row_x, c)
+    for i in range(count):
+        if i == AHEAD:
+            send_panel(0, row_x)
+        send_green(i)
 
     def pairs(body):
         if cols == PAIR:
@@ -153,12 +162,6 @@
     pass_on(1)
     for k in range(cols):
         start(slab_x.at[c, 1, k], column.at[row_x * cols + c], late_sent, late_recv, row_y, k)
-    pass_on(0)
-    arrived(far_in, far_recv)
-    to_x[...] = (to_x[...].astype(jnp.float32) + far_in[...].astype(jnp.float32)).astype(jnp.bfloat16)
-    for k in range(cols):
-        start(to_x.at[k], xsum.at[c], x_sent, x_recv, row_x, k)
-
     def send_sum(i):
         low, high = chunks[i]
         span = pl.ds(low, high - low)
@@ -207,14 +210,22 @@
         arrived(column.at[group(row_far)], late_recv)
 
     shared(1)
-    send_sum(0)
-    shared(0)
-    keep_sum(0)
-    for s in range(cols):
-        column[r * cols + s] = slab[s, me]
-        column[row_x * cols + s] = slab_x[s, 0, c]
-    for i in range(1, count):
+    for i in range(AHEAD):
         send_sum(i)
+    arrived(far_in, far_recv)
+    to_x[...] = (to_x[...].astype(jnp.float32) + far_in[...].astype(jnp.float32)).astype(jnp.bfloat16)
+    for k in range(cols):
+        start(to_x.at[k], xsum.at[c], x_sent, x_recv, row_x, k)
+    pass_on(0)
+    for i in range(AHEAD, count):
+        send_sum(i)
+        if i == AHEAD:
+            shared(0)
+            for s in range(cols):
+                column[r * cols + s] = slab[s, me]
+                column[row_x * cols + s] = slab_x[s, 0, c]
+            for h in range(AHEAD):
+                keep_sum(h)
         keep_sum(i)
         if i >= LAG:
             if i == LAG:

time: 23.4 us -> 23.4 us (level)
  no operation moved by 1% of the time
where the time goes in v5:
time: 23.4 us; the launch traced here: 23.2 us
  Pallas kernels  22.6 us (97%)
  between operations  0.64 us (3%)
    pallas_call x1, Pallas kernels, local(): pl.pallas_call(functools.partial(exchange, rows, cols), out_shape=(pltpu....  21.8 us
    pallas_call x1, Pallas kernels, local(): pl.pallas_call(store, out_shape=(jax.ShapeDtypeStruct((cols * total, widt...  0.78 us

profile of v5, /device:TPU:0, one launch (start us, length us, event | category | flops | bytes accessed | tf_op | source)
XLA Modules:
  0.0 23.2 jit_solution(12449839752397705835)
XLA Ops:
  0.6 21.8 %shard_map.59 = (bf16[1536,128]{1,0:T(8,128)(2,1)S(1)}, f32[128,128]{1,0:T(8,128)S(1)}) custom-call(s32[8,12]{1,0:T(8,128)} %bitcast.7, bf16[768,384]{1,0:T(8,128)(2,1)} %bitcast.5, bf16[192,8,128]{2,1,0:T(8,128)(2,1)} %panel_hbm.1, f32[128,128]{1,0:T(8,128)} %bitcast.6), custom_call_target="tpu_custom_call" | custom-call | tf_op jit(solution)/shard_map/pallas_call | solution.py:290
  22.5 0.8 %shard_map.60 = (bf16[1536,128]{1,0:T(8,128)(2,1)}, f32[128,128]{1,0:T(8,128)}) custom-call(bf16[1536,128]{1,0:T(8,128)(2,1)S(1)} %get-tuple-element.6.made, f32[128,128]{1,0:T(8,128)S(1)} %get-tuple-element.7.grown), custom_call_target="tpu_custom_call" | custom-call | tf_op jit(solution)/shard_map/pallas_call | solution.py:305
